TPU v7x, 512 devices: a whole 4x4x16 slice. The times are simulated.
512 devices in a mesh: cls: 8 (over z_lo, core), ptcl: 64 (over y, z_hi, x).
Axes of the slice: x: 4, y: 4, z: 16 (z_hi: 4, z_lo: 4; z = z_hi * 4 + z_lo), core: 2. Of those that a mesh axis runs over, the one named last changes fastest.
Arguments:
- particles: bfloat16 [65536, 2048], P('ptcl')
- panels: bfloat16 [8, 128, 2048], P('cls', 'ptcl')
- sigma2: float32 [32], replicated, may hold values from 0.5 to 2
- defocus_bins: int32 [65536], P('ptcl'), may hold values from 0 to 15
- half_sets: int32 [65536], P('ptcl'), may hold values 0 or 1
- prior_mask: int32 [65536, 8], P('ptcl', 'cls'), may hold values from 0 to 1, as said below
- orient_ids: int32 [128], replicated, may hold values from 0 to 127, each once
Outputs:
- half_maps: float32 [8, 256, 2048], P('cls', 'ptcl')
- log_evidence: float32 [65536], P('ptcl')
Inputs may be any that keep to these rules, and one draw needn't show every extreme that they name: `prior_mask`: every particle allows at least one class. `orient_ids`: each direction 0 to 127 appears once.
All inputs are finite; a program needn't handle non-finite values. No bound on the sum of `half_sets` on one device may be relied on, other than what follows from the above.
Results may differ from a plain program's by a relative error of at most 0.0015.
The roundings to bfloat16 on the way count: a program that leaves them out, or rounds other values in their place, can miss the bound.
Values may be sent and summed in bfloat16 or wider, within the bound.
No kernel may reach another device: no remote copies, remote signals or barrier semaphores. Data moves between devices by JAX's collectives and lax.ppermute only.
A program may use at most 64 MiB of HBM per device.

v0:
```python
import jax
import jax.numpy as jnp
from jax import lax
from jax.sharding import PartitionSpec as P

PIXC = 1024
ORIENT = 128
NSHELL = 32
NBIN = 16


def from_partner(shard, axis, apart):
    return lax.ppermute(shard, axis, [(i, i ^ 1 << apart) for i in range(lax.axis_size(axis))])


def ctf_table():
    bins = jnp.arange(NBIN, dtype=jnp.float32)
    defocus = (bins + 1.0) / NBIN
    radius = (jnp.arange(PIXC, dtype=jnp.float32) + 0.5) / PIXC
    phase = 0.3 + 2.5 * defocus[:, None] * radius[None, :]
    return jnp.sin(phase) + 0.1 * jnp.cos(phase)


def lookup_small(indices, values):
    count = values.shape[0]
    match = indices[:, None] == jnp.arange(count, dtype=jnp.int32)[None, :]
    return jnp.sum(jnp.where(match, values[None, :], 0.0), axis=1)


def contract_rows(left, right):
    return lax.dot_general(
        left, right, (((0,), (0,)), ((), ())), preferred_element_type=jnp.float32
    )


def on_device(particles, panels, sigma2, defocus_bins, half_sets, prior_mask, orient_ids):
    shells = jnp.arange(PIXC, dtype=jnp.int32) * NSHELL // PIXC
    inverse_noise = lookup_small(shells, 1.0 / sigma2)
    table = ctf_table()
    onehot_bin = (defocus_bins[:, None] == jnp.arange(NBIN, dtype=jnp.int32)[None, :]).astype(
        jnp.float32
    )
    contrast = jnp.dot(onehot_bin, table, precision=lax.Precision.HIGHEST)
    doubled = jnp.concatenate([contrast, contrast], axis=1)
    noise_pair = jnp.concatenate([inverse_noise, inverse_noise])
    images = particles.astype(jnp.float32)
    weighted = (images * doubled * noise_pair[None, :]).astype(jnp.bfloat16)
    power = (contrast * contrast * inverse_noise[None, :]).astype(jnp.bfloat16)
    piece = lax.all_gather(panels[0], "ptcl", axis=0, tiled=True)
    piece_f = piece.astype(jnp.float32)
    piece_power = (piece_f[:, :PIXC] ** 2 + piece_f[:, PIXC:] ** 2).astype(jnp.bfloat16)
    direct = lax.dot_general(
        weighted, piece, (((1,), (1,)), ((), ())), preferred_element_type=jnp.float32
    )
    norm_part = lax.dot_general(
        power, piece_power, (((1,), (1,)), ((), ())), preferred_element_type=jnp.float32
    )
    scores = direct - 0.5 * norm_part
    allowed = (prior_mask[:, 0] > 0)[:, None]
    masked = jnp.where(allowed, scores, -1e30)
    local_peak = jnp.max(masked, axis=1)
    peak = lax.pmax(local_peak, "cls")
    weights_exp = jnp.where(allowed, jnp.exp(masked - peak[:, None]), 0.0)
    total = lax.psum(jnp.sum(weights_exp, axis=1), "cls")
    log_evidence = peak + jnp.log(total)
    posterior = (weights_exp / total[:, None]).astype(jnp.bfloat16)
    permuter = (orient_ids[:, None] == jnp.arange(ORIENT, dtype=jnp.int32)[None, :]).astype(
        jnp.bfloat16
    )
    by_direction = jnp.dot(posterior, permuter, preferred_element_type=jnp.float32).astype(
        jnp.bfloat16
    )
    half_col = half_sets.astype(jnp.bfloat16)[:, None]
    split_post = jnp.concatenate([by_direction * (1 - half_col), by_direction * half_col], axis=1)
    centred = (images * doubled).astype(jnp.bfloat16)
    squares_ctf = (contrast * contrast).astype(jnp.bfloat16)
    stacked = jnp.concatenate([centred, squares_ctf], axis=1)
    summed = lax.psum_scatter(
        contract_rows(split_post, stacked), "ptcl", scatter_dimension=0, tiled=True
    )
    data = summed[:, : 2 * PIXC]
    weight = summed[:, 2 * PIXC :]
    top_bit = lax.axis_size("ptcl").bit_length() - 2
    partner = from_partner(data.astype(jnp.bfloat16), "ptcl", top_bit).astype(data.dtype)
    half_index = lax.axis_index("ptcl") // (lax.axis_size("ptcl") // 2)

    def per_shell(values):
        summed_rows = jnp.sum(values, axis=0)
        folded = summed_rows[:PIXC] + summed_rows[PIXC:]
        return jnp.sum(folded.reshape(NSHELL, PIXC // NSHELL), axis=1)

    cross = per_shell(data * partner)
    own_power = per_shell(data * data)
    is_first = half_index == 0
    stats = jnp.stack(
        [0.5 * cross, jnp.where(is_first, own_power, 0.0), jnp.where(is_first, 0.0, own_power)]
    )
    totals = lax.psum(stats, "ptcl")
    fsc = totals[0] / jnp.sqrt(totals[1] * totals[2] + 1e-06)
    factor = (1.0 + lookup_small(shells, fsc)) / 2.0
    factor_pair = jnp.concatenate([factor, factor])
    weight_pair = jnp.concatenate([weight, weight], axis=1)
    half_maps = data * factor_pair[None, :] / (weight_pair + 1.0)
    return (half_maps[None], log_evidence)


def solution(mesh):
    placed = (
        P("ptcl", None),
        P("cls", "ptcl", None),
        P(),
        P("ptcl"),
        P("ptcl"),
        P("ptcl", "cls"),
        P(),
    )
    return jax.shard_map(
        on_device,
        mesh=mesh,
        in_specs=placed,
        out_specs=(P("cls", "ptcl", None), P("ptcl")),
        check_vma=False,
    )
```

profile of v0, /device:TPU:32, one launch (start us, length us, event | category | flops | bytes accessed | tf_op | source)
XLA Modules:
  0.0 1377.2 jit_solution(9083316655074497782)
XLA Ops:
  7.2 0.0 all-reduce.3.cloned.1.call-start
  7.3 0.7 broadcast_divide_fusion
  7.9 0.1 select_reduce_fusion.1
  8.0 0.0 copy-start.1
  8.0 0.0 copy-start.2
  8.0 6.4 copy.14
  14.5 0.0 copy-done.1
  14.5 234.2 %all-gather = bf16[1,128,2048]{2,0,1:T(2,128)(2,1)S(1)} all-gather(bf16[1,2,2048]{2,0,1:T(2,128)(2,1)S(1)} %copy.15), channel_id=2, replica_groups=mesh['cls'=8,'ptcl'=64] {'ptcl'}, dimensions={1}, use_global_device_ids=true | all-gather | bytes 532480 | tf_op jit(solution)/shard_map/all_gather | solution.py:49
  248.7 0.0 copy-start
  248.7 0.4 bitcast_convert_fusion
  249.0 0.0 copy-done.2
  249.1 2.2 multiply_convert_fusion.3
  251.3 0.0 copy-done
  251.3 3.3 fusion
  254.6 0.0 copy-start.3
  254.6 1.5 fusion.5
  256.1 0.0 copy-done.3
  256.1 0.0 copy-start.4
  256.1 0.0 copy-start.5
  256.2 0.7 fusion.46
  256.9 10.0 pmax.7
  266.9 0.1 fusion.18
  267.0 13.5 psum.14
  280.5 0.0 copy-done.4
  280.5 0.0 copy-done.5
  280.5 0.3 broadcast_multiply_fusion.1
  280.9 5.8 fusion.1
  286.7 0.0 all-reduce.3.cloned.1.call-update
  286.7 1.3 dynamic-slice
  288.6 848.2 %all-reduce.3.cloned.1.call-done = f32[256,3072]{1,0:T(8,128)} async-done(((f32[256,3072]{1,0:T(8,128)}), f32[256,3072]{1,0:T(8,128)}) %all-reduce.3.cloned.1.call-update) | async-done | bytes 3145744
  1136.8 0.8 dynamic-slice_convert_fusion
  1137.6 1.9 collective-permute-start
  1139.5 0.6 log_add_fusion
  1140.2 0.8 dynamic-slice.3
  1141.0 3.8 collective-permute-done
  1144.8 0.9 multiply_reduce_fusion.1
  1145.7 0.1 add.87
  1145.7 0.1 add.85
  1145.8 0.1 reduce_sum.68
  1145.9 0.1 reduce_sum.66
  1146.1 222.7 %psum.15 = f32[3,32]{1,0:T(4,128)S(1)} all-reduce(f32[3,32]{1,0:T(4,128)S(1)} %pad_maximum_fusion.2), channel_id=1, replica_groups=mesh['cls'=8,'ptcl'=64] {'ptcl'}, use_global_device_ids=true, to_apply=%region_10.11 | all-reduce | flops 96 | bytes 768 | tf_op jit(solution)/shard_map/psum | solution.py:98
  1368.8 0.1 select_reduce_fusion
  1368.9 1.5 fusion.35
  (14 shorter events, 0.1 us)
Async XLA Ops:
  7.2 1129.6 %all-reduce.3.cloned.1.call-start = ((), (), s32[]{:S(2)}) async-start(), calls=%async_computation | async-start | bytes 6291456
  8.0 6.4 copy-start.1
  8.0 241.0 %copy-start.2 = (s32[1024]{0:T(1024)S(1)}, s32[1024]{0:T(1024)}, u32[]{:S(2)}) copy-start(s32[1024]{0:T(1024)} %param.10) | copy-start | bytes 12292
  248.7 2.6 copy-start
  254.6 1.5 copy-start.3
  256.1 24.4 %copy-start.4 = (s32[1024]{0:T(1024)S(1)}, s32[1024]{0:T(1024)}, u32[]{:S(2)}) copy-start(s32[1024]{0:T(1024)} %param.11) | copy-start | bytes 12292
  256.1 24.4 %copy-start.5 = (s32[128]{0:T(128)S(1)}, s32[128]{0:T(128)}, u32[]{:S(2)}) copy-start(s32[128]{0:T(128)} %param.13) | copy-start | bytes 1540
  1137.6 7.1 collective-permute-start
Sparse Core Ops, SparseCore 0:
  286.8 849.9 all-reduce.2
where the time goes:
time: 1380 us
  waiting for transfers between devices  852 us (62%)
  blocking collectives  480 us (35%)
  between operations  14.9 us (1%)
    unnamed x2, waiting for transfers between devices  848 us
    all_gather x1, blocking collectives, on_device(): piece = lax.all_gather(panels[0], 'ptcl', axis=0, tiled=True)  234 us
    psum x1, blocking collectives, on_device(): totals = lax.psum(stats, 'ptcl')  223 us
  transfers between devices with their start and end apart: 2, of which 2 were waited for; matrix products, arithmetic and copies ran while one was open for 0% of the time, Pallas kernels for 0%

commit v1 on v0

--- a/solution.py
+++ b/solution.py
@@ -46,7 +46,9 @@
     images = particles.astype(jnp.float32)
     weighted = (images * doubled * noise_pair[None, :]).astype(jnp.bfloat16)
     power = (contrast * contrast * inverse_noise[None, :]).astype(jnp.bfloat16)
-    piece = lax.all_gather(panels[0], "ptcl", axis=0, tiled=True)
+    piece = jnp.concatenate(
+        lax.all_to_all(jnp.stack([panels[0]] * lax.axis_size("ptcl")), "ptcl", 0, 0), axis=0
+    )
     piece_f = piece.astype(jnp.float32)
     piece_power = (piece_f[:, :PIXC] ** 2 + piece_f[:, PIXC:] ** 2).astype(jnp.bfloat16)
     direct = lax.dot_general(

time: 1380 us -> 1200 us (0.87)
  blocking collectives: 480 us -> 244 us
  waiting for transfers between devices: 852 us -> 879 us
  starting transfers between devices: 1.96 us -> 22.3 us
    all_gather x1 -> x0, blocking collectives: 234 us -> none  [on_device(): piece = lax.all_gather(panels[0], 'ptcl', axis=0, tiled=True)]
    all_to_all x0 -> x1, waiting for transfers between devices: none -> 22.2 us  [on_device(): lax.all_to_all(jnp.stack([panels[0]] * lax.axis_size('ptcl')), 'ptcl', 0, 0)]
    all_to_all x0 -> x1, starting transfers between devices: none -> 20.3 us  [on_device(): lax.all_to_all(jnp.stack([panels[0]] * lax.axis_size('ptcl')), 'ptcl', 0, 0)]
  transfers between devices with their start and end apart: 2 -> 3, of which waited for: 2 -> 3; matrix products, arithmetic and copies ran while one was open for 0% -> 1% of each run, Pallas kernels for 0% -> 0%
where the time goes in v1:
time: 1200 us
  waiting for transfers between devices  879 us (73%)
  blocking collectives  244 us (20%)
  starting transfers between devices  22.3 us (2%)
  between operations  14.9 us (1%)
  matrix products  14.5 us (1%)
  local copies, waits for them, and re-layouts  13.8 us (1%)
    unnamed x2, waiting for transfers between devices  853 us
    psum x1, blocking collectives, on_device(): totals = lax.psum(stats, 'ptcl')  223 us
  transfers between devices with their start and end apart: 3, of which 3 were waited for; matrix products, arithmetic and copies ran while one was open for 1% of the time, Pallas kernels for 0%

profile of v1, /device:TPU:32, one launch (start us, length us, event | category | flops | bytes accessed | tf_op | source)
XLA Modules:
  0.0 1195.9 jit_solution(12878862586434508725)
XLA Ops:
  7.2 1.8 stack.4
  9.0 20.3 %all-to-all-start = ((bf16[64,2,2048]{2,1,0:T(2,128)(2,1)}), bf16[64,2,2048]{2,1,0:T(2,128)(2,1)S(1)}, u32[]{:S(2)}, u32[]{:S(2)}) async-start(bf16[64,2,2048]{2,1,0:T(2,128)(2,1)} %stack.4), calls=%async_computation | async-start | bytes 1048576 | tf_op jit(solution)/shard_map/all_to_all | solution.py:50
  29.3 0.0 all-reduce.3.cloned.1.call-start
  29.3 0.0 copy-start.6
  29.3 0.0 copy-start.4
  29.3 0.0 copy-start.5
  29.4 0.0 copy-start.3
  29.4 6.4 copy.11
  35.8 0.0 copy-start.2
  35.8 0.0 copy-done.6
  35.8 0.1 select_reduce_fusion.1
  35.9 0.0 copy-done.4
  36.0 0.0 copy-done.5
  36.0 0.0 copy-done.3
  36.0 2.2 multiply_convert_fusion.3
  38.2 0.0 copy-start
  38.3 2.0 copy-done
  40.2 0.0 copy-done.2
  40.2 3.2 fusion
  43.5 22.2 %all-to-all-done = bf16[64,2,2048]{2,1,0:T(2,128)(2,1)S(1)} async-done(((bf16[64,2,2048]{2,1,0:T(2,128)(2,1)}), bf16[64,2,2048]{2,1,0:T(2,128)(2,1)S(1)}, u32[]{:S(2)}, u32[]{:S(2)}) %all-to-all-start) | async-done | bytes 524320 | tf_op jit(solution)/shard_map/all_to_all | solution.py:50
  65.7 0.2 reshape.114
  65.9 0.1 convert_element_type.41
  66.0 0.0 copy-start.1
  66.0 5.5 fusion.5
  71.5 0.3 copy-done.1
  71.8 0.7 fusion.44
  72.6 10.6 pmax.7
  83.2 0.1 fusion.17
  83.3 10.8 psum.14
  94.1 0.0 copy-done.7
  94.1 0.3 broadcast_multiply_fusion.1
  94.4 5.7 fusion.1
  100.2 0.0 all-reduce.3.cloned.1.call-update
  100.2 1.3 dynamic-slice
  102.1 853.3 %all-reduce.3.cloned.1.call-done = f32[256,3072]{1,0:T(8,128)} async-done(((f32[256,3072]{1,0:T(8,128)}), f32[256,3072]{1,0:T(8,128)}) %all-reduce.3.cloned.1.call-update) | async-done | bytes 3145744
  955.4 0.8 dynamic-slice_convert_fusion
  956.3 1.9 collective-permute-start
  958.2 0.6 log_add_fusion
  958.8 0.8 dynamic-slice.3
  959.6 3.8 collective-permute-done
  963.4 0.9 multiply_reduce_fusion.1
  964.3 0.1 add.87
  964.4 0.1 add.85
  964.4 0.1 reduce_sum.68
  964.6 0.1 reduce_sum.66
  964.7 222.7 %psum.15 = f32[3,32]{1,0:T(4,128)S(1)} all-reduce(f32[3,32]{1,0:T(4,128)S(1)} %pad_maximum_fusion.2), channel_id=1, replica_groups=mesh['cls'=8,'ptcl'=64] {'ptcl'}, use_global_device_ids=true, to_apply=%region_10.11 | all-reduce | flops 96 | bytes 768 | tf_op jit(solution)/shard_map/psum | solution.py:100
  1187.4 0.1 select_reduce_fusion
  1187.5 1.5 fusion.33
  (15 shorter events, 0.1 us)
Async XLA Ops:
  9.0 56.7 %all-to-all-start = ((bf16[64,2,2048]{2,1,0:T(2,128)(2,1)}), bf16[64,2,2048]{2,1,0:T(2,128)(2,1)S(1)}, u32[]{:S(2)}, u32[]{:S(2)}) async-start(bf16[64,2,2048]{2,1,0:T(2,128)(2,1)} %stack.4), calls=%async_computation | async-start | bytes 1048576 | tf_op jit(solution)/shard_map/all_to_all | solution.py:50
  29.3 926.1 %all-reduce.3.cloned.1.call-start = ((), (), s32[]{:S(2)}) async-start(), calls=%async_computation.1 | async-start | bytes 6291456
  29.3 6.5 copy-start.6
  29.3 6.6 copy-start.4
  29.3 6.6 copy-start.5
  29.4 6.6 copy-start.3
  35.8 4.4 copy-start.2
  38.2 2.0 copy-start
  66.0 5.8 copy-start.1
  71.8 22.2 %copy-start.7 = (s32[128]{0:T(128)S(1)}, s32[128]{0:T(128)}, u32[]{:S(2)}) copy-start(s32[128]{0:T(128)} %param.13) | copy-start | bytes 1540
  956.3 7.1 collective-permute-start
Sparse Core Ops, SparseCore 0:
  100.3 855.0 all-reduce.2
